TPU v7x, 256 devices: a whole 4x4x8 slice. The times are simulated.
256 devices in a mesh: seq: 64 (over y, z, core), ch: 4 (over x).
Axes of the slice: x: 4, y: 4, z: 8, core: 2. Of those that a mesh axis runs over, the one named last changes fastest.
Arguments:
- features: bfloat16 [32768, 1024], P('seq', 'ch'), may hold values from -6 to 6
- w_in: bfloat16 [1024, 3, 1024], P(None, None, 'ch'), may hold values from -0.1875 to 0.1875
- bias_skip: float32 [1024], P('ch'), may hold values from -3 to 3
- filters: float32 [32768, 1024], P('seq', 'ch')
- w_out: bfloat16 [1024, 1024], P(None, 'ch'), may hold values from -0.1875 to 0.1875
- w_emb: bfloat16 [1024, 128], P('ch'), may hold values from -0.1875 to 0.1875
- page_lengths: int32 [512], replicated, may hold values from 1 to 256, 32768 in all
- page_owner: int32 [512], replicated, may hold values from 0 to 63
Outputs:
- index_rows: bfloat16 [32768, 128], P('seq')
Inputs may be any that keep to these rules, and one draw needn't show every extreme that they name: page_lengths sum to 32768, and the longest page has exactly 256 patches.
All inputs are finite; a program needn't handle non-finite values.
Results may differ from a plain program's by a relative error of at most 0.0057.
Values may be sent and summed in bfloat16 or wider, within the bound.
A program may use at most 64 MiB of HBM per device.

v0:
```python
import math
import jax
import jax.numpy as jnp
from jax import lax
from jax.sharding import PartitionSpec as P


def angle_table(first_index, second_index, period):
    product = first_index[:, None] * second_index[None, :] % period
    return product.astype(jnp.float32) * (2.0 * math.pi / period)


def apply_table(table, values):
    return jnp.einsum("ki,qic->qkc", table, values, precision=lax.Precision.HIGHEST)


def long_convolution(signal, filters, seq_count, seq_rank):
    rows_dev, chan_dev = signal.shape
    group_rows = rows_dev // seq_count
    block_count = 2 * seq_count
    fft_length = block_count * rows_dev
    block_index = jnp.arange(block_count, dtype=jnp.int32)
    source_index = jnp.arange(seq_count, dtype=jnp.int32)
    outer_angle = angle_table(block_index, source_index, block_count)
    outer_cos = jnp.cos(outer_angle)
    outer_sin = jnp.sin(outer_angle)
    local_rows = seq_rank * group_rows + jnp.arange(group_rows, dtype=jnp.int32)
    twist_angle = angle_table(block_index, local_rows, fft_length)
    twist_cos = jnp.cos(twist_angle)[:, :, None]
    twist_sin = jnp.sin(twist_angle)[:, :, None]
    inner_index = jnp.arange(rows_dev, dtype=jnp.int32)
    inner_angle = angle_table(inner_index, inner_index, rows_dev)
    inner_cos = jnp.cos(inner_angle)
    inner_sin = jnp.sin(inner_angle)
    signal_blocks, filter_blocks = (
        lax.all_to_all(
            signal.reshape(seq_count, group_rows, chan_dev),
            "seq",
            split_axis=0,
            concat_axis=0,
            tiled=True,
        ),
        lax.all_to_all(
            filters.reshape(seq_count, group_rows, chan_dev),
            "seq",
            split_axis=0,
            concat_axis=0,
            tiled=True,
        ),
    )

    def outer_forward(blocks):
        real_part = jnp.einsum("kj,jic->kic", outer_cos, blocks, precision=lax.Precision.HIGHEST)
        imag_part = -jnp.einsum("kj,jic->kic", outer_sin, blocks, precision=lax.Precision.HIGHEST)
        return jnp.stack(
            [
                real_part * twist_cos + imag_part * twist_sin,
                imag_part * twist_cos - real_part * twist_sin,
            ]
        )

    signal_spec, filter_spec = (
        lax.all_to_all(
            outer_forward(signal_blocks), "seq", split_axis=1, concat_axis=2, tiled=True
        ),
        lax.all_to_all(
            outer_forward(filter_blocks), "seq", split_axis=1, concat_axis=2, tiled=True
        ),
    )

    def inner_forward(spectrum):
        real_in = spectrum[0]
        imag_in = spectrum[1]
        return (
            apply_table(inner_cos, real_in) + apply_table(inner_sin, imag_in),
            apply_table(inner_cos, imag_in) - apply_table(inner_sin, real_in),
        )

    signal_real, signal_imag = inner_forward(signal_spec)
    filter_real, filter_imag = inner_forward(filter_spec)
    product_real = signal_real * filter_real - signal_imag * filter_imag
    product_imag = signal_real * filter_imag + signal_imag * filter_real
    back_real = apply_table(inner_cos, product_real) - apply_table(inner_sin, product_imag)
    back_imag = apply_table(inner_cos, product_imag) + apply_table(inner_sin, product_real)
    returned = lax.all_to_all(
        jnp.stack([back_real, back_imag]), "seq", split_axis=2, concat_axis=1, tiled=True
    )
    turned_real = returned[0] * twist_cos - returned[1] * twist_sin
    turned_imag = returned[0] * twist_sin + returned[1] * twist_cos
    result = (
        jnp.einsum("kj,kic->jic", outer_cos, turned_real, precision=lax.Precision.HIGHEST)
        - jnp.einsum("kj,kic->jic", outer_sin, turned_imag, precision=lax.Precision.HIGHEST)
    ) / fft_length
    back_tokens = lax.all_to_all(result, "seq", split_axis=0, concat_axis=1, tiled=True)
    return back_tokens.reshape(rows_dev, chan_dev)


def source_tokens(page_lengths, page_owner, output_rows):
    page_index = jnp.arange(page_lengths.shape[0], dtype=jnp.int32)
    before = (page_owner[None, :] < page_owner[:, None]) | (
        page_owner[None, :] == page_owner[:, None]
    ) & (page_index[None, :] < page_index[:, None])
    placed_start = jnp.sum(jnp.where(before, page_lengths[None, :], 0), axis=1)
    page_start = jnp.cumsum(page_lengths) - page_lengths
    inside = (output_rows[:, None] >= placed_start[None, :]) & (
        output_rows[:, None] < (placed_start + page_lengths)[None, :]
    )
    offsets = page_start[None, :] + output_rows[:, None] - placed_start[None, :]
    return jnp.sum(jnp.where(inside, offsets, 0), axis=1)


def body(features, w_in, bias_skip, filters, w_out, w_emb, page_lengths, page_owner):
    rows_dev, chan_dev = features.shape
    seq_count = lax.axis_size("seq")
    seq_rank = lax.axis_index("seq")
    flat_in = w_in.reshape(w_in.shape[0], -1)
    weight_rows = flat_in
    projected = jnp.dot(
        lax.all_gather(features, "ch", axis=1, tiled=True),
        weight_rows,
        preferred_element_type=jnp.float32,
    )
    projected = projected.reshape(rows_dev, 3, chan_dev)
    gate_branch = projected[:, 0]
    signal = projected[:, 1] * projected[:, 2]
    convolved = long_convolution(signal, filters, seq_count, seq_rank)
    mixed = ((convolved + bias_skip[None, :] * signal) * gate_branch).astype(jnp.bfloat16)
    weight_rows = w_out
    summed = jnp.dot(
        lax.all_gather(mixed, "ch", axis=1, tiled=True),
        weight_rows,
        preferred_element_type=jnp.float32,
    )
    layer_out = (summed + features.astype(jnp.float32)).astype(jnp.bfloat16)
    output_rows = seq_rank * rows_dev + jnp.arange(rows_dev, dtype=jnp.int32)
    source = source_tokens(page_lengths, page_owner, output_rows)
    embedded = lax.psum(jnp.dot(layer_out, w_emb, preferred_element_type=jnp.float32), "ch").astype(
        jnp.bfloat16
    )
    shard_part = lax.all_gather(embedded, "seq", axis=0, tiled=True)
    count_rows = shard_part.shape[0]
    inside = (source >= 0) & (source < count_rows)
    taken = jnp.take(shard_part, jnp.clip(source, 0, count_rows - 1), axis=0)
    return jnp.where(inside[:, None], taken, jnp.zeros_like(embedded))


def solution(mesh):
    return jax.shard_map(
        body,
        mesh=mesh,
        in_specs=(
            P("seq", "ch"),
            P(None, None, "ch"),
            P("ch"),
            P("seq", "ch"),
            P(None, "ch"),
            P("ch", None),
            P(),
            P(),
        ),
        out_specs=P("seq", None),
        check_vma=False,
    )
```

profile of v0, /device:TPU:1, one launch (start us, length us, event | category | flops | bytes accessed | tf_op | source)
XLA Modules:
  0.0 488.9 jit_solution(5704225290694879429)
XLA Ops:
  7.3 13.2 %all-to-all-start.2 = ((f32[64,8,256]{2,1,0:T(8,128)}), f32[64,8,256]{2,1,0:T(8,128)S(1)}, u32[]{:S(2)}, u32[]{:S(2)}) async-start(f32[64,8,256]{2,1,0:T(8,128)} %bitcast.145), calls=%async_computation.2 | async-start | bytes 1048576 | tf_op jit(solution)/shard_map/all_to_all | solution.py:43
  22.1 17.4 %all-gather.4.cloned.1.call-done = bf16[512,1024]{1,0:T(8,128)(2,1)} async-done(((bf16[512,256]{1,0:T(8,128)(2,1)}), bf16[512,1024]{1,0:T(8,128)(2,1)}) %all-gather.4.cloned.1.call-update) | async-done | bytes 1048592 | tf_op jit(solution)/shard_map/all_gather | solution.py:119
  43.9 12.0 %all-to-all-start = ((f32[64,8,256]{2,1,0:T(8,128)}), f32[64,8,256]{2,1,0:T(8,128)S(1)}, u32[]{:S(2)}, u32[]{:S(2)}) async-start(f32[64,8,256]{2,1,0:T(8,128)} %fusion.89), calls=%async_computation | async-start | bytes 1048576 | tf_op jit(solution)/shard_map/all_to_all | solution.py:36
  59.4 13.8 %all-to-all-done = f32[64,8,256]{2,1,0:T(8,128)S(1)} async-done(((f32[64,8,256]{2,1,0:T(8,128)}), f32[64,8,256]{2,1,0:T(8,128)S(1)}, u32[]{:S(2)}, u32[]{:S(2)}) %all-to-all-start) | async-done | bytes 524320 | tf_op jit(solution)/shard_map/all_to_all | solution.py:36
  80.0 6.8 %all-to-all-start.3 = ((f32[2,128,8,256]{3,2,0,1:T(8,128)}), f32[2,128,8,256]{3,2,0,1:T(8,128)S(1)}, u32[]{:S(2)}, u32[]{:S(2)}) async-start(f32[2,128,8,256]{3,2,0,1:T(8,128)} %copy.64), calls=%async_computation.3 | async-start | bytes 4194304 | tf_op jit(solution)/shard_map/all_to_all | solution.py:66
  91.0 46.9 %all-to-all-done.3 = f32[2,128,8,256]{3,2,0,1:T(8,128)S(1)} async-done(((f32[2,128,8,256]{3,2,0,1:T(8,128)}), f32[2,128,8,256]{3,2,0,1:T(8,128)S(1)}, u32[]{:S(2)}, u32[]{:S(2)}) %all-to-all-start.3) | async-done | bytes 2097184 | tf_op jit(solution)/shard_map/all_to_all | solution.py:66
  147.0 7.2 %fusion.16 = f32[2,256,512]{2,1,0:T(8,128)S(1)} fusion(f32[1,2,64,8,256]{4,3,1,2,0:T(8,128)S(1)} %get-tuple-element.13), kind=kOutput, calls=%fused_computation.34 | convolution fusion | flops 1614282752 | bytes 2097152 | tf_op jit(solution)/shard_map/ki,qic->qkc/dot_general | solution.py:14
  154.2 7.4 %fusion.20 = f32[2,256,512]{2,1,0:T(8,128)S(1)} fusion(f32[1,2,64,8,256]{4,3,1,2,0:T(8,128)S(1)} %get-tuple-element.14), kind=kOutput, calls=%fused_computation.38 | convolution fusion | flops 1614282752 | bytes 2097152 | tf_op jit(solution)/shard_map/ki,qic->qkc/dot_general | solution.py:14
  161.6 8.1 %convolution_subtract_fusion.1 = f32[2,256,512]{2,1,0:T(8,128)} fusion(f32[2,256,512]{2,1,0:T(8,128)S(1)} %fusion.16, f32[1,2,64,8,256]{4,3,1,2,0:T(8,128)S(1)} %get-tuple-element.14), kind=kOutput, calls=%fused_computation.16 | convolution fusion | flops 1614544896 | bytes 3145728 | tf_op jit(solution)/shard_map/ki,qic->qkc/dot_general | solution.py:14
  169.7 8.3 %convolution_add_fusion.1 = f32[2,256,512]{2,1,0:T(8,128)} fusion(f32[2,256,512]{2,1,0:T(8,128)S(1)} %fusion.20, f32[1,2,64,8,256]{4,3,1,2,0:T(8,128)S(1)} %get-tuple-element.13), kind=kOutput, calls=%fused_computation.18 | convolution fusion | flops 1614544896 | bytes 3145728 | tf_op jit(solution)/shard_map/ki,qic->qkc/dot_general | solution.py:14
  178.0 18.3 %all-to-all-done.1 = f32[2,128,8,256]{3,2,0,1:T(8,128)S(1)} async-done(((f32[2,128,8,256]{3,2,0,1:T(8,128)}), f32[2,128,8,256]{3,2,0,1:T(8,128)S(1)}, u32[]{:S(2)}, u32[]{:S(2)}) %all-to-all-start.1) | async-done | bytes 2097184 | tf_op jit(solution)/shard_map/all_to_all | solution.py:63
  196.6 7.2 %fusion.36 = f32[2,256,512]{2,1,0:T(8,128)S(1)} fusion(f32[1,2,64,8,256]{4,3,1,2,0:T(8,128)S(1)} %get-tuple-element.15), kind=kOutput, calls=%fused_computation.54 | convolution fusion | flops 1614282752 | bytes 2097152 | tf_op jit(solution)/shard_map/ki,qic->qkc/dot_general | solution.py:14
  203.8 7.6 %fusion.28 = f32[2,256,512]{2,1,0:T(8,128)S(1)} fusion(f32[1,2,64,8,256]{4,3,1,2,0:T(8,128)S(1)} %get-tuple-element.16), kind=kOutput, calls=%fused_computation.46 | convolution fusion | flops 1614282752 | bytes 2097152 | tf_op jit(solution)/shard_map/ki,qic->qkc/dot_general | solution.py:14
  211.4 7.2 %convolution_add_fusion.2 = f32[2,256,512]{2,1,0:T(8,128)S(1)} fusion(f32[2,256,512]{2,1,0:T(8,128)S(1)} %fusion.36, f32[1,2,64,8,256]{4,3,1,2,0:T(8,128)S(1)} %get-tuple-element.16), kind=kOutput, calls=%fused_computation.19 | convolution fusion | flops 1614544896 | bytes 3145728 | tf_op jit(solution)/shard_map/ki,qic->qkc/dot_general | solution.py:14
  218.6 7.6 %multiply_subtract_fusion = (f32[2,256,512]{2,1,0:T(8,128)S(1)}, f32[2,256,512]{2,1,0:T(8,128)S(1)}) fusion(f32[2,256,512]{2,1,0:T(8,128)S(1)} %copy-done.5, f32[2,256,512]{2,1,0:T(8,128)S(1)} %convolution_add_fusion.2, f32[2,256,512]{2,1,0:T(8,128)S(1)} %copy-done.6, f32[2,256,512]{2,1,0:T(8,128)S(1)} %fusion.28, ...), kind=kOutput, calls=%fused_computation.67 | convolution fusion | flops 1616117760 | bytes 7340032 | tf_op jit(solution)/shard_map/ki,qic->qkc/dot_general | solution.py:14
  226.2 6.3 %fusion.14 = f32[2,256,512]{2,1,0:T(8,128)S(1)} fusion(f32[2,256,512]{2,1,0:T(8,128)S(1)} %get-tuple-element.5), kind=kOutput, calls=%fused_computation.32 | convolution fusion | flops 1614282752 | bytes 2097152 | tf_op jit(solution)/shard_map/ki,qic->qkc/dot_general | solution.py:14
  232.6 6.5 %fusion.10 = f32[2,256,512]{2,1,0:T(8,128)S(1)} fusion(f32[2,256,512]{2,1,0:T(8,128)S(1)} %get-tuple-element.6), kind=kOutput, calls=%fused_computation.28 | convolution fusion | flops 1614282752 | bytes 2097152 | tf_op jit(solution)/shard_map/ki,qic->qkc/dot_general | solution.py:14
  239.1 6.3 %fusion.3 = f32[1,2,512,256]{2,3,1,0:T(8,128)S(1)} fusion(f32[2,256,512]{2,1,0:T(8,128)S(1)} %fusion.14, f32[2,256,512]{2,1,0:T(8,128)S(1)} %get-tuple-element.6), kind=kOutput, calls=%fused_computation.15 | convolution fusion | flops 1614544896 | bytes 3145728 | tf_op jit(solution)/shard_map/ki,qic->qkc/dot_general | solution.py:14
  245.5 6.3 %fusion.2 = f32[1,2,512,256]{2,3,1,0:T(8,128)S(1)} fusion(f32[2,256,512]{2,1,0:T(8,128)S(1)} %fusion.10, f32[2,256,512]{2,1,0:T(8,128)S(1)} %get-tuple-element.5), kind=kOutput, calls=%fused_computation.13 | convolution fusion | flops 1614544896 | bytes 3145728 | tf_op jit(solution)/shard_map/ki,qic->qkc/dot_general | solution.py:14
  254.5 57.4 %all_to_all.64 = f32[2,2,512,256]{3,1,0,2:T(2,128)S(1)} all-to-all(f32[2,2,512,256]{3,1,0,2:T(2,128)} %copy.74), channel_id=1, replica_groups=mesh['seq'=64,'ch'=4] {'seq'}, dimensions={2} | all-to-all | bytes 4194304 | tf_op jit(solution)/shard_map/all_to_all | solution.py:85
  322.2 23.0 %all_to_all.65 = f32[64,8,256]{2,1,0:T(8,128)S(1)} all-to-all(f32[64,8,256]{2,1,0:T(8,128)S(1)} %copy.78), channel_id=1, replica_groups=mesh['seq'=64,'ch'=4] {'seq'}, dimensions={0} | all-to-all | bytes 1048576 | tf_op jit(solution)/shard_map/all_to_all | solution.py:94
  346.1 23.0 %all-gather.6.cloned.1.call-done = bf16[512,1024]{1,0:T(8,128)(2,1)} async-done(((bf16[512,256]{1,0:T(8,128)(2,1)}), bf16[512,1024]{1,0:T(8,128)(2,1)}) %all-gather.6.cloned.1.call-update) | async-done | bytes 1048592 | tf_op jit(solution)/shard_map/all_gather | solution.py:130
  371.0 15.8 %all-reduce.1 = bf16[512,128]{1,0:T(8,128)(2,1)} all-reduce(f32[512,128]{1,0:T(8,128)S(1)} %fusion.6), channel_id=1, replica_groups=mesh['seq'=64,'ch'=4] {'ch'}, use_global_device_ids=true, to_apply=%region_4.5 | all-reduce | flops 65536 | bytes 393216 | tf_op jit(solution)/shard_map/psum | solution.py:137
  388.2 87.3 %all-gather.8.cloned.1.call-done = bf16[32768,128]{1,0:T(8,128)(2,1)} async-done(((bf16[512,128]{1,0:T(8,128)(2,1)}), bf16[32768,128]{1,0:T(8,128)(2,1)}) %all-gather.8.cloned.1.call-update) | async-done | bytes 8388624 | tf_op jit(solution)/shard_map/all_gather | solution.py:140
  (75 shorter events, 54.1 us)
Async XLA Ops:
  6.5 362.6 %copy-start = (bf16[1024,256]{1,0:T(8,128)(2,1)S(1)}, bf16[1024,256]{1,0:T(8,128)(2,1)}, u32[]{:S(2)}) copy-start(bf16[1024,256]{1,0:T(8,128)(2,1)} %param.12) | copy-start | bytes 1572868
  6.5 33.0 %all-gather.4.cloned.1.call-start = ((), (), s32[]{:S(2)}) async-start(), calls=%async_computation.6 | async-start | bytes 1310720 | tf_op jit(solution)/shard_map/all_gather | solution.py:119
  7.3 36.6 %all-to-all-start.2 = ((f32[64,8,256]{2,1,0:T(8,128)}), f32[64,8,256]{2,1,0:T(8,128)S(1)}, u32[]{:S(2)}, u32[]{:S(2)}) async-start(f32[64,8,256]{2,1,0:T(8,128)} %bitcast.145), calls=%async_computation.2 | async-start | bytes 1048576 | tf_op jit(solution)/shard_map/all_to_all | solution.py:43
  41.8 1.2 copy-start.2
  43.9 29.3 %all-to-all-start = ((f32[64,8,256]{2,1,0:T(8,128)}), f32[64,8,256]{2,1,0:T(8,128)S(1)}, u32[]{:S(2)}, u32[]{:S(2)}) async-start(f32[64,8,256]{2,1,0:T(8,128)} %fusion.89), calls=%async_computation | async-start | bytes 1048576 | tf_op jit(solution)/shard_map/all_to_all | solution.py:36
  73.2 1.2 copy-start.4
  80.0 57.9 %all-to-all-start.3 = ((f32[2,128,8,256]{3,2,0,1:T(8,128)}), f32[2,128,8,256]{3,2,0,1:T(8,128)S(1)}, u32[]{:S(2)}, u32[]{:S(2)}) async-start(f32[2,128,8,256]{3,2,0,1:T(8,128)} %copy.64), calls=%async_computation.3 | async-start | bytes 4194304 | tf_op jit(solution)/shard_map/all_to_all | solution.py:66
  138.0 1.3 copy-start.1
  139.3 57.0 %all-to-all-start.1 = ((f32[2,128,8,256]{3,2,0,1:T(8,128)}), f32[2,128,8,256]{3,2,0,1:T(8,128)S(1)}, u32[]{:S(2)}, u32[]{:S(2)}) async-start(f32[2,128,8,256]{3,2,0,1:T(8,128)} %copy.56), calls=%async_computation.1 | async-start | bytes 4194304 | tf_op jit(solution)/shard_map/all_to_all | solution.py:63
  145.0 224.1 %all-gather.6.cloned.1.call-start = ((), (), s32[]{:S(2)}) async-start(), calls=%async_computation.7 | async-start | bytes 1310720 | tf_op jit(solution)/shard_map/all_gather | solution.py:130
  211.4 7.2 %copy-start.5 = (f32[2,256,512]{2,1,0:T(8,128)S(1)}, f32[2,256,512]{2,1,0:T(8,128)}, u32[]{:S(2)}) copy-start(f32[2,256,512]{2,1,0:T(8,128)} %convolution_subtract_fusion.1) | copy-start | bytes 3145732
  211.4 7.2 %copy-start.6 = (f32[2,256,512]{2,1,0:T(8,128)S(1)}, f32[2,256,512]{2,1,0:T(8,128)}, u32[]{:S(2)}) copy-start(f32[2,256,512]{2,1,0:T(8,128)} %convolution_add_fusion.1) | copy-start | bytes 3145732
  320.9 24.3 %copy-start.3 = (f32[512,3,256]{2,0,1:T(8,128)S(1)}, f32[512,3,256]{2,0,1:T(8,128)}, u32[]{:S(2)}) copy-start(f32[512,3,256]{2,0,1:T(8,128)} %copy-done.2) | copy-start | bytes 4718596
  320.9 24.3 %copy-start.10 = (f32[256]{0:T(256)S(1)}, f32[256]{0:T(256)}, u32[]{:S(2)}) copy-start(f32[256]{0:T(256)} %param.10) | copy-start | bytes 3076
  322.2 46.9 %copy-start.7 = (bf16[512,256]{1,0:T(8,128)(2,1)S(1)}, bf16[512,256]{1,0:T(8,128)(2,1)}, u32[]{:S(2)}) copy-start(bf16[512,256]{1,0:T(8,128)(2,1)} %param.8) | copy-start | bytes 786436
  322.2 46.9 %copy-start.11 = (bf16[256,128]{1,0:T(8,128)(2,1)S(1)}, bf16[256,128]{1,0:T(8,128)(2,1)}, u32[]{:S(2)}) copy-start(bf16[256,128]{1,0:T(8,128)(2,1)} %param.13) | copy-start | bytes 196612
  346.0 40.8 %copy-start.8 = (s32[512]{0:T(512)S(1)}, s32[512]{0:T(512)}, u32[]{:S(2)}) copy-start(s32[512]{0:T(512)} %param.14) | copy-start | bytes 6148
  346.0 41.3 %copy-start.9 = (s32[512]{0:T(512)S(1)}, s32[512]{0:T(512)}, u32[]{:S(2)}) copy-start(s32[512]{0:T(512)} %param.15) | copy-start | bytes 6148
  346.1 129.5 %all-gather.8.cloned.1.call-start = ((), (), s32[]{:S(2)}) async-start(), calls=%async_computation.8 | async-start | bytes 8519680 | tf_op jit(solution)/shard_map/all_gather | solution.py:140
Sparse Core Ops, SparseCore 0:
  9.1 30.3 all-gather.3
  346.2 22.8 all-gather.5
  386.9 88.5 all-gather.7
where the time goes:
time: 498 us; the launch traced here: 489 us
  waiting for transfers between devices  207 us (42%)
  matrix products  99.6 us (20%)
  blocking collectives  96.2 us (19%)
  starting transfers between devices  37.7 us (8%)
  local copies, waits for them, and re-layouts  28.1 us (6%)
  between operations  13.9 us (3%)
  other arithmetic  5.95 us (1%)
    all_gather x1, waiting for transfers between devices, body(): shard_part = lax.all_gather(embedded, 'seq', axis=0, tiled=True)  87.3 us
    dot_general x12, matrix products, apply_table(): jnp.einsum('ki,qic->qkc', table, values, precision=lax.Precision.HIGHEST)  86.1 us
    all_to_all x1, blocking collectives, long_convolution(): lax.all_to_all(jnp.stack([back_real, back_imag]), 'seq', split_axis=2, co...  57.4 us
    all_to_all x1, waiting for transfers between devices, long_convolution(): lax.all_to_all(outer_forward(filter_blocks), 'seq', split_axis=1, concat_...  46.9 us
    all_gather x1, waiting for transfers between devices, body(): lax.all_gather(mixed, 'ch', axis=1, tiled=True)  23 us
    all_to_all x1, blocking collectives, long_convolution(): lax.all_to_all(result, 'seq', split_axis=0, concat_axis=1, tiled=True)  23 us
    all_to_all x1, waiting for transfers between devices, long_convolution(): lax.all_to_all(outer_forward(signal_blocks), 'seq', split_axis=1, concat_...  18.3 us
    all_gather x1, waiting for transfers between devices, body(): lax.all_gather(features, 'ch', axis=1, tiled=True)  17.4 us
  transfers between devices with their start and end apart: 7, of which 6 were waited for; matrix products, arithmetic and copies ran while one was open for 10% of the time, Pallas kernels for 0%

commit v1 on v0

--- a/solution.py
+++ b/solution.py
@@ -137,7 +137,9 @@
     embedded = lax.psum(jnp.dot(layer_out, w_emb, preferred_element_type=jnp.float32), "ch").astype(
         jnp.bfloat16
     )
-    shard_part = lax.all_gather(embedded, "seq", axis=0, tiled=True)
+    shard_part = jnp.concatenate(
+        lax.all_to_all(jnp.stack([embedded] * lax.axis_size("seq")), "seq", 0, 0), axis=0
+    )
     count_rows = shard_part.shape[0]
     inside = (source >= 0) & (source < count_rows)
     taken = jnp.take(shard_part, jnp.clip(source, 0, count_rows - 1), axis=0)

time: 498 us -> 623 us (1.25)
  waiting for transfers between devices: 207 us -> 311 us
  starting transfers between devices: 37.7 us -> 53.9 us
    all_to_all x0 -> x1, waiting for transfers between devices: none -> 184 us  [body(): lax.all_to_all(jnp.stack([embedded] * lax.axis_size('seq')), 'seq', 0, 0)]
    all_gather x1 -> x0, waiting for transfers between devices: 87.3 us -> none  [body(): shard_part = lax.all_gather(embedded, 'seq', axis=0, tiled=True)]
    all_to_all x0 -> x1, starting transfers between devices: none -> 16.4 us  [body(): lax.all_to_all(jnp.stack([embedded] * lax.axis_size('seq')), 'seq', 0, 0)]
    all_to_all x1, waiting for transfers between devices: 18.3 us -> 25.3 us  [long_convolution(): lax.all_to_all(outer_forward(signal_blocks), 'seq', split_axis=1, concat_...]
  transfers between devices with their start and end apart: 7 -> 7, of which waited for: 6 -> 6; matrix products, arithmetic and copies ran while one was open for 10% -> 6% of each run, Pallas kernels for 0% -> 0%
where the time goes in v1:
time: 623 us; the launch traced here: 615 us
  waiting for transfers between devices  311 us (50%)
  matrix products  100 us (16%)
  blocking collectives  95.9 us (15%)
  starting transfers between devices  53.9 us (9%)
  local copies, waits for them, and re-layouts  33.4 us (5%)
  between operations  14.3 us (2%)
    all_to_all x1, waiting for transfers between devices, body(): lax.all_to_all(jnp.stack([embedded] * lax.axis_size('seq')), 'seq', 0, 0)  184 us
    dot_general x12, matrix products, apply_table(): jnp.einsum('ki,qic->qkc', table, values, precision=lax.Precision.HIGHEST)  86.6 us
    all_to_all x1, blocking collectives, long_convolution(): lax.all_to_all(jnp.stack([back_real, back_imag]), 'seq', split_axis=2, co...  57 us
    all_to_all x1, waiting for transfers between devices, long_convolution(): lax.all_to_all(outer_forward(filter_blocks), 'seq', split_axis=1, concat_...  46.9 us
    all_to_all x1, waiting for transfers between devices, long_convolution(): lax.all_to_all(outer_forward(signal_blocks), 'seq', split_axis=1, concat_...  25.3 us
    all_to_all x1, blocking collectives, long_convolution(): lax.all_to_all(result, 'seq', split_axis=0, concat_axis=1, tiled=True)  23.5 us
    all_gather x1, waiting for transfers between devices, body(): lax.all_gather(mixed, 'ch', axis=1, tiled=True)  22.9 us
    all_gather x1, waiting for transfers between devices, body(): lax.all_gather(features, 'ch', axis=1, tiled=True)  17.4 us
  transfers between devices with their start and end apart: 7, of which 6 were waited for; matrix products, arithmetic and copies ran while one was open for 6% of the time, Pallas kernels for 0%

profile of v1, /device:TPU:1, one launch (start us, length us, event | category | flops | bytes accessed | tf_op | source)
XLA Modules:
  0.0 614.7 jit_solution(1548636594959899292)
XLA Ops:
  7.3 13.2 %all-to-all-start.2 = ((f32[64,8,256]{2,1,0:T(8,128)}), f32[64,8,256]{2,1,0:T(8,128)S(1)}, u32[]{:S(2)}, u32[]{:S(2)}) async-start(f32[64,8,256]{2,1,0:T(8,128)} %bitcast.146), calls=%async_computation.2 | async-start | bytes 1048576 | tf_op jit(solution)/shard_map/all_to_all | solution.py:43
  22.1 17.4 %all-gather.3.cloned.1.call-done = bf16[512,1024]{1,0:T(8,128)(2,1)} async-done(((bf16[512,256]{1,0:T(8,128)(2,1)}), bf16[512,1024]{1,0:T(8,128)(2,1)}) %all-gather.3.cloned.1.call-update) | async-done | bytes 1048592 | tf_op jit(solution)/shard_map/all_gather | solution.py:119
  43.9 12.0 %all-to-all-start = ((f32[64,8,256]{2,1,0:T(8,128)}), f32[64,8,256]{2,1,0:T(8,128)S(1)}, u32[]{:S(2)}, u32[]{:S(2)}) async-start(f32[64,8,256]{2,1,0:T(8,128)} %fusion.89), calls=%async_computation | async-start | bytes 1048576 | tf_op jit(solution)/shard_map/all_to_all | solution.py:36
  59.4 13.8 %all-to-all-done = f32[64,8,256]{2,1,0:T(8,128)S(1)} async-done(((f32[64,8,256]{2,1,0:T(8,128)}), f32[64,8,256]{2,1,0:T(8,128)S(1)}, u32[]{:S(2)}, u32[]{:S(2)}) %all-to-all-start) | async-done | bytes 524320 | tf_op jit(solution)/shard_map/all_to_all | solution.py:36
  80.0 6.6 %all-to-all-start.3 = ((f32[2,128,8,256]{3,2,0,1:T(8,128)}), f32[2,128,8,256]{3,2,0,1:T(8,128)S(1)}, u32[]{:S(2)}, u32[]{:S(2)}) async-start(f32[2,128,8,256]{3,2,0,1:T(8,128)} %copy.64), calls=%async_computation.3 | async-start | bytes 4194304 | tf_op jit(solution)/shard_map/all_to_all | solution.py:66
  90.9 46.9 %all-to-all-done.3 = f32[2,128,8,256]{3,2,0,1:T(8,128)S(1)} async-done(((f32[2,128,8,256]{3,2,0,1:T(8,128)}), f32[2,128,8,256]{3,2,0,1:T(8,128)S(1)}, u32[]{:S(2)}, u32[]{:S(2)}) %all-to-all-start.3) | async-done | bytes 2097184 | tf_op jit(solution)/shard_map/all_to_all | solution.py:66
  146.9 7.2 %fusion.20 = f32[2,256,512]{2,1,0:T(8,128)S(1)} fusion(f32[1,2,64,8,256]{4,3,1,2,0:T(8,128)S(1)} %get-tuple-element.14), kind=kOutput, calls=%fused_computation.38 | convolution fusion | flops 1614282752 | bytes 2097152 | tf_op jit(solution)/shard_map/ki,qic->qkc/dot_general | solution.py:14
  154.1 8.5 %fusion.16 = f32[2,256,512]{2,1,0:T(8,128)} fusion(f32[1,2,64,8,256]{4,3,1,2,0:T(8,128)S(1)} %get-tuple-element.13), kind=kOutput, calls=%fused_computation.34 | convolution fusion | flops 1614282752 | bytes 2097152 | tf_op jit(solution)/shard_map/ki,qic->qkc/dot_general | solution.py:14
  162.6 8.2 %convolution_add_fusion.1 = f32[2,256,512]{2,1,0:T(8,128)} fusion(f32[2,256,512]{2,1,0:T(8,128)S(1)} %fusion.20, f32[1,2,64,8,256]{4,3,1,2,0:T(8,128)S(1)} %get-tuple-element.13), kind=kOutput, calls=%fused_computation.18 | convolution fusion | flops 1614544896 | bytes 3145728 | tf_op jit(solution)/shard_map/ki,qic->qkc/dot_general | solution.py:14
  170.8 25.3 %all-to-all-done.1 = f32[2,128,8,256]{3,2,0,1:T(8,128)S(1)} async-done(((f32[2,128,8,256]{3,2,0,1:T(8,128)}), f32[2,128,8,256]{3,2,0,1:T(8,128)S(1)}, u32[]{:S(2)}, u32[]{:S(2)}) %all-to-all-start.1) | async-done | bytes 2097184 | tf_op jit(solution)/shard_map/all_to_all | solution.py:63
  196.4 7.2 %fusion.36 = f32[2,256,512]{2,1,0:T(8,128)S(1)} fusion(f32[1,2,64,8,256]{4,3,1,2,0:T(8,128)S(1)} %get-tuple-element.15), kind=kOutput, calls=%fused_computation.54 | convolution fusion | flops 1614282752 | bytes 2097152 | tf_op jit(solution)/shard_map/ki,qic->qkc/dot_general | solution.py:14
  203.6 7.4 %fusion.28 = f32[2,256,512]{2,1,0:T(8,128)S(1)} fusion(f32[1,2,64,8,256]{4,3,1,2,0:T(8,128)S(1)} %get-tuple-element.16), kind=kOutput, calls=%fused_computation.46 | convolution fusion | flops 1614282752 | bytes 2097152 | tf_op jit(solution)/shard_map/ki,qic->qkc/dot_general | solution.py:14
  211.0 7.2 %convolution_add_fusion.2 = f32[2,256,512]{2,1,0:T(8,128)S(1)} fusion(f32[2,256,512]{2,1,0:T(8,128)S(1)} %fusion.36, f32[1,2,64,8,256]{4,3,1,2,0:T(8,128)S(1)} %get-tuple-element.16), kind=kOutput, calls=%fused_computation.19 | convolution fusion | flops 1614544896 | bytes 3145728 | tf_op jit(solution)/shard_map/ki,qic->qkc/dot_general | solution.py:14
  218.3 7.6 %convolution_subtract_fusion.1 = f32[2,256,512]{2,1,0:T(8,128)S(1)} fusion(f32[2,256,512]{2,1,0:T(8,128)S(1)} %copy-done.13, f32[1,2,64,8,256]{4,3,1,2,0:T(8,128)S(1)} %copy-done.7), kind=kOutput, calls=%fused_computation.16 | convolution fusion | flops 1614544896 | bytes 3145728 | tf_op jit(solution)/shard_map/ki,qic->qkc/dot_general | solution.py:14
  226.0 7.6 %multiply_subtract_fusion = (f32[2,256,512]{2,1,0:T(8,128)S(1)}, f32[2,256,512]{2,1,0:T(8,128)S(1)}) fusion(f32[2,256,512]{2,1,0:T(8,128)S(1)} %convolution_subtract_fusion.1, f32[2,256,512]{2,1,0:T(8,128)S(1)} %convolution_add_fusion.2, f32[2,256,512]{2,1,0:T(8,128)S(1)} %copy-done.5, f32[2,256,512]{2,1,0:T(8,128)S(1)} %fusion.28, ...), kind=kOutput, calls=%fused_computation.67 | convolution fusion | flops 1616117760 | bytes 7340032 | tf_op jit(solution)/shard_map/ki,qic->qkc/dot_general | solution.py:14
  239.9 6.3 %fusion.10 = f32[2,256,512]{2,1,0:T(8,128)S(1)} fusion(f32[2,256,512]{2,1,0:T(8,128)S(1)} %get-tuple-element.6), kind=kOutput, calls=%fused_computation.28 | convolution fusion | flops 1614282752 | bytes 2097152 | tf_op jit(solution)/shard_map/ki,qic->qkc/dot_general | solution.py:14
  246.2 6.3 %fusion.3 = f32[1,2,512,256]{2,3,1,0:T(8,128)S(1)} fusion(f32[2,256,512]{2,1,0:T(8,128)S(1)} %fusion.14, f32[2,256,512]{2,1,0:T(8,128)S(1)} %get-tuple-element.6), kind=kOutput, calls=%fused_computation.15 | convolution fusion | flops 1614544896 | bytes 3145728 | tf_op jit(solution)/shard_map/ki,qic->qkc/dot_general | solution.py:14
  252.6 6.6 %fusion.2 = f32[1,2,512,256]{2,3,1,0:T(8,128)S(1)} fusion(f32[2,256,512]{2,1,0:T(8,128)S(1)} %fusion.10, f32[2,256,512]{2,1,0:T(8,128)S(1)} %get-tuple-element.5), kind=kOutput, calls=%fused_computation.13 | convolution fusion | flops 1614544896 | bytes 3145728 | tf_op jit(solution)/shard_map/ki,qic->qkc/dot_general | solution.py:14
  261.8 57.0 %all_to_all.69 = f32[2,2,512,256]{3,1,0,2:T(2,128)S(1)} all-to-all(f32[2,2,512,256]{3,1,0,2:T(2,128)} %copy.74), channel_id=1, replica_groups=mesh['seq'=64,'ch'=4] {'seq'}, dimensions={2} | all-to-all | bytes 4194304 | tf_op jit(solution)/shard_map/all_to_all | solution.py:85
  329.2 23.5 %all_to_all.70 = f32[64,8,256]{2,1,0:T(8,128)S(1)} all-to-all(f32[64,8,256]{2,1,0:T(8,128)S(1)} %copy.78), channel_id=1, replica_groups=mesh['seq'=64,'ch'=4] {'seq'}, dimensions={0} | all-to-all | bytes 1048576 | tf_op jit(solution)/shard_map/all_to_all | solution.py:94
  353.5 22.9 %all-gather.5.cloned.1.call-done = bf16[512,1024]{1,0:T(8,128)(2,1)} async-done(((bf16[512,256]{1,0:T(8,128)(2,1)}), bf16[512,1024]{1,0:T(8,128)(2,1)}) %all-gather.5.cloned.1.call-update) | async-done | bytes 1048592 | tf_op jit(solution)/shard_map/all_gather | solution.py:130
  378.3 15.4 %all-reduce.1 = bf16[512,128]{1,0:T(8,128)(2,1)S(1)} all-reduce(f32[512,128]{1,0:T(8,128)S(1)} %fusion.6), channel_id=1, replica_groups=mesh['seq'=64,'ch'=4] {'ch'}, use_global_device_ids=true, to_apply=%region_4.5 | all-reduce | flops 65536 | bytes 393216 | tf_op jit(solution)/shard_map/psum | solution.py:137
  398.9 16.4 %all-to-all-start.6 = ((bf16[64,512,128]{2,1,0:T(8,128)(2,1)}), bf16[64,512,128]{2,1,0:T(8,128)(2,1)}, u32[]{:S(2)}, u32[]{:S(2)}) async-start(bf16[64,512,128]{2,1,0:T(8,128)(2,1)} %stack.29), calls=%async_computation.6 | async-start | bytes 16777216 | tf_op jit(solution)/shard_map/all_to_all | solution.py:141
  416.7 184.3 %all-to-all-done.6 = bf16[64,512,128]{2,1,0:T(8,128)(2,1)} async-done(((bf16[64,512,128]{2,1,0:T(8,128)(2,1)}), bf16[64,512,128]{2,1,0:T(8,128)(2,1)}, u32[]{:S(2)}, u32[]{:S(2)}) %all-to-all-start.6) | async-done | bytes 8388640 | tf_op jit(solution)/shard_map/all_to_all | solution.py:141
  (79 shorter events, 65.6 us)
Async XLA Ops:
  6.5 369.9 %copy-start = (bf16[1024,256]{1,0:T(8,128)(2,1)S(1)}, bf16[1024,256]{1,0:T(8,128)(2,1)}, u32[]{:S(2)}) copy-start(bf16[1024,256]{1,0:T(8,128)(2,1)} %param.12) | copy-start | bytes 1572868
  6.5 33.0 %all-gather.3.cloned.1.call-start = ((), (), s32[]{:S(2)}) async-start(), calls=%async_computation.7 | async-start | bytes 1310720 | tf_op jit(solution)/shard_map/all_gather | solution.py:119
  7.3 36.6 %all-to-all-start.2 = ((f32[64,8,256]{2,1,0:T(8,128)}), f32[64,8,256]{2,1,0:T(8,128)S(1)}, u32[]{:S(2)}, u32[]{:S(2)}) async-start(f32[64,8,256]{2,1,0:T(8,128)} %bitcast.146), calls=%async_computation.2 | async-start | bytes 1048576 | tf_op jit(solution)/shard_map/all_to_all | solution.py:43
  41.8 1.2 copy-start.2
  43.9 29.3 %all-to-all-start = ((f32[64,8,256]{2,1,0:T(8,128)}), f32[64,8,256]{2,1,0:T(8,128)S(1)}, u32[]{:S(2)}, u32[]{:S(2)}) async-start(f32[64,8,256]{2,1,0:T(8,128)} %fusion.89), calls=%async_computation | async-start | bytes 1048576 | tf_op jit(solution)/shard_map/all_to_all | solution.py:36
  73.2 1.2 copy-start.4
  80.0 57.8 %all-to-all-start.3 = ((f32[2,128,8,256]{3,2,0,1:T(8,128)}), f32[2,128,8,256]{3,2,0,1:T(8,128)S(1)}, u32[]{:S(2)}, u32[]{:S(2)}) async-start(f32[2,128,8,256]{3,2,0,1:T(8,128)} %copy.64), calls=%async_computation.3 | async-start | bytes 4194304 | tf_op jit(solution)/shard_map/all_to_all | solution.py:66
  137.8 1.3 copy-start.1
  139.1 57.0 %all-to-all-start.1 = ((f32[2,128,8,256]{3,2,0,1:T(8,128)}), f32[2,128,8,256]{3,2,0,1:T(8,128)S(1)}, u32[]{:S(2)}, u32[]{:S(2)}) async-start(f32[2,128,8,256]{3,2,0,1:T(8,128)} %copy.56), calls=%async_computation.1 | async-start | bytes 4194304 | tf_op jit(solution)/shard_map/all_to_all | solution.py:63
  144.9 231.5 %all-gather.5.cloned.1.call-start = ((), (), s32[]{:S(2)}) async-start(), calls=%async_computation.8 | async-start | bytes 1310720 | tf_op jit(solution)/shard_map/all_gather | solution.py:130
  146.8 7.2 %copy-start.6 = (f32[1,2,64,8,256]{4,3,1,2,0:T(8,128)}, f32[1,2,64,8,256]{4,3,1,2,0:T(8,128)S(1)}, u32[]{:S(2)}) copy-start(f32[1,2,64,8,256]{4,3,1,2,0:T(8,128)S(1)} %get-tuple-element.14) | copy-start | bytes 3145732
  211.0 7.3 %copy-start.7 = (f32[1,2,64,8,256]{4,3,1,2,0:T(8,128)S(1)}, f32[1,2,64,8,256]{4,3,1,2,0:T(8,128)}, u32[]{:S(2)}) copy-start(f32[1,2,64,8,256]{4,3,1,2,0:T(8,128)} %copy-done.6) | copy-start | bytes 3145732
  211.0 7.3 %copy-start.13 = (f32[2,256,512]{2,1,0:T(8,128)S(1)}, f32[2,256,512]{2,1,0:T(8,128)}, u32[]{:S(2)}) copy-start(f32[2,256,512]{2,1,0:T(8,128)} %fusion.16) | copy-start | bytes 3145732
  218.3 7.6 %copy-start.5 = (f32[2,256,512]{2,1,0:T(8,128)S(1)}, f32[2,256,512]{2,1,0:T(8,128)}, u32[]{:S(2)}) copy-start(f32[2,256,512]{2,1,0:T(8,128)} %convolution_add_fusion.1) | copy-start | bytes 3145732
  327.9 24.8 %copy-start.3 = (f32[512,3,256]{2,0,1:T(8,128)S(1)}, f32[512,3,256]{2,0,1:T(8,128)}, u32[]{:S(2)}) copy-start(f32[512,3,256]{2,0,1:T(8,128)} %copy-done.2) | copy-start | bytes 4718596
  327.9 24.8 %copy-start.11 = (f32[256]{0:T(256)S(1)}, f32[256]{0:T(256)}, u32[]{:S(2)}) copy-start(f32[256]{0:T(256)} %param.10) | copy-start | bytes 3076
  329.2 47.2 %copy-start.8 = (bf16[512,256]{1,0:T(8,128)(2,1)S(1)}, bf16[512,256]{1,0:T(8,128)(2,1)}, u32[]{:S(2)}) copy-start(bf16[512,256]{1,0:T(8,128)(2,1)} %param.8) | copy-start | bytes 786436
  329.2 47.2 %copy-start.12 = (bf16[256,128]{1,0:T(8,128)(2,1)S(1)}, bf16[256,128]{1,0:T(8,128)(2,1)}, u32[]{:S(2)}) copy-start(bf16[256,128]{1,0:T(8,128)(2,1)} %param.13) | copy-start | bytes 196612
  398.9 16.4 %copy-start.9 = (s32[512]{0:T(512)S(1)}, s32[512]{0:T(512)}, u32[]{:S(2)}) copy-start(s32[512]{0:T(512)} %param.14) | copy-start | bytes 6148
  398.9 16.9 %copy-start.10 = (s32[512]{0:T(512)S(1)}, s32[512]{0:T(512)}, u32[]{:S(2)}) copy-start(s32[512]{0:T(512)} %param.15) | copy-start | bytes 6148
  398.9 202.1 %all-to-all-start.6 = ((bf16[64,512,128]{2,1,0:T(8,128)(2,1)}), bf16[64,512,128]{2,1,0:T(8,128)(2,1)}, u32[]{:S(2)}, u32[]{:S(2)}) async-start(bf16[64,512,128]{2,1,0:T(8,128)(2,1)} %stack.29), calls=%async_computation.6 | async-start | bytes 16777216 | tf_op jit(solution)/shard_map/all_to_all | solution.py:141
Sparse Core Ops, SparseCore 0:
  9.1 30.3 all-gather.2
  353.7 22.7 all-gather.4
